TPU v7x, 256 devices: a whole 4x4x8 slice. The times are simulated.
256 devices in a mesh: dp: 32 (over x, y, core), tp: 8 (over z).
Axes of the slice: x: 4, y: 4, z: 8, core: 2. Of those that a mesh axis runs over, the one named last changes fastest.
Arguments:
- arrived_rows: bfloat16 [12288, 7168], P('dp', 'tp'), may hold values from -6 to 6
- row_counts: int32 [32], P('dp'), may hold values from 1 to 384, 4096 in all
- routes: int32 [4096, 8], P('dp'), may hold values from 0 to 31, all different within a row; in each aligned block of 128 rows (0 to 127, 128 to 255, ...) at most 40 rows name the same one
- gate_scale: float32 [4096, 8], P('dp'), may hold values from 0.1 to 0.6
- w_gate: bfloat16 [32, 7168, 1024], P('dp', 'tp'), may hold values from -0.0625 to 0.0625
- w_up: bfloat16 [32, 7168, 1024], P('dp', 'tp'), may hold values from -0.0625 to 0.0625
- w_down: bfloat16 [32, 1024, 7168], P('dp', None, 'tp'), may hold values from -0.1875 to 0.1875
- cotangent: bfloat16 [4096, 7168], P('dp', 'tp'), may hold values from -6 to 6
Outputs:
- layer_out: bfloat16 [4096, 7168], P('dp', 'tp')
- grad_rows: bfloat16 [12288, 7168], P('dp', 'tp')
Inputs may be any that keep to these rules, and one draw needn't show every extreme that they name: `row_counts`: the counts sum to exactly 4096; the largest is exactly 384. `routes`: each row names 8 different experts; within the 128 rows of one index of dp no expert is named by more than 40 rows, a bound that some block reaches.
All inputs are finite; a program needn't handle non-finite values. No bound on the sum of `row_counts` on one device may be relied on, other than what follows from the above.
Results may differ from a plain program's by a relative error of at most 0.03.
Values may be sent and summed in bfloat16 or wider, within the bound.
No kernel may reach another device: no remote copies, remote signals or barrier semaphores. Data moves between devices by JAX's collectives and lax.ppermute only.
A program may use at most 64 MiB of HBM per device.

v0:
```python
import jax
import jax.numpy as jnp
from jax import lax
from jax.sharding import PartitionSpec as P

BF = jnp.bfloat16
F32 = jnp.float32


def rounded(tensor):
    return lax.optimization_barrier(tensor.astype(BF))


def select(left, right):
    return jnp.dot(left, right, preferred_element_type=F32).astype(BF)


def select_t(left, right):
    return lax.dot_general(
        left, right, (((0,), (0,)), ((), ())), preferred_element_type=F32
    ).astype(BF)


def dot_nt(left, right):
    return lax.dot_general(left, right, (((1,), (1,)), ((), ())), preferred_element_type=F32)


def on_device(arrived_rows, row_counts, routes, gate_scale, w_gate, w_up, w_down, cotangent):
    members = lax.axis_size("dp")
    myself = lax.axis_index("dp")
    slot_count, part = arrived_rows.shape
    rows, top = routes.shape
    capacity = rows * top // members + rows * top // (4 * members)
    per_peer = -(-(slot_count // members) // 16) * 16
    gate_proj, up_proj, down_proj = (w_gate[0], w_up[0], w_down[0])

    def exchange(tensor):
        return lax.all_to_all(tensor, "dp", split_axis=0, concat_axis=0, tiled=True)

    ids = jnp.arange(members, dtype=jnp.int32)
    chosen = routes.T[None, :, :] == ids[:, None, None]
    named = jnp.any(chosen, axis=1)
    before = jnp.arange(rows)[:, None] < jnp.arange(rows)[None, :]
    place = jnp.dot(named.astype(BF), before.astype(BF), preferred_element_type=F32)
    place = jnp.where(named, place.astype(jnp.int32), -1)
    slots = jnp.arange(capacity, dtype=jnp.int32)
    hot = place[:, None, :] == slots[None, :, None]
    pack = hot.astype(BF).reshape(members * capacity, rows)
    shipped_grad = exchange(select(pack, cotangent).reshape(members, capacity, part))
    all_counts = lax.all_gather(row_counts, "dp", axis=0, tiled=True)
    starts = jnp.sum(jnp.where(ids[None, :] < ids[:, None], all_counts[None, :], 0), axis=1)
    my_start = starts[myself]
    my_count = all_counts[myself]
    column = jnp.arange(per_peer, dtype=jnp.int32)
    source_slot = (ids[:, None] - my_start) % members + column[None, :] * members
    source_slot = jnp.where(source_slot < my_count, source_slot, -1).reshape(-1)
    spread = (source_slot[:, None] == jnp.arange(slot_count, dtype=jnp.int32)[None, :]).astype(BF)
    incoming = exchange(select(spread, arrived_rows).reshape(members, per_peer, part))
    offset = (jnp.arange(rows, dtype=jnp.int32) * members + myself)[:, None] - starts[None, :]
    held = (offset >= 0) & (offset < all_counts[None, :])
    taken = jnp.where(held, offset // members, -1)
    take = (taken[:, :, None] == column[None, None, :]).astype(BF).reshape(rows, -1)
    balanced = select(take, incoming.reshape(-1, part))
    shipped = exchange(select(pack, balanced).reshape(members, capacity, part))
    grad_part = rounded(dot_nt(shipped_grad.reshape(-1, part), down_proj))
    hidden_grad = lax.psum_scatter(grad_part, "tp", scatter_dimension=0, tiled=True)
    flat = shipped.reshape(-1, part)
    gate_part = rounded(jnp.dot(flat, gate_proj, preferred_element_type=F32))
    up_part = rounded(jnp.dot(flat, up_proj, preferred_element_type=F32))
    gate_pre = lax.psum_scatter(gate_part, "tp", scatter_dimension=0, tiled=True)
    up_pre = lax.psum_scatter(up_part, "tp", scatter_dimension=0, tiled=True)
    gate_pre, up_pre, hidden_grad = (v.astype(F32) for v in (gate_pre, up_pre, hidden_grad))
    sigmoid_gate = jax.nn.sigmoid(gate_pre)
    hidden = (gate_pre * sigmoid_gate * up_pre).astype(BF)
    gate_grad = (
        hidden_grad * up_pre * sigmoid_gate * (1.0 + gate_pre * (1.0 - sigmoid_gate))
    ).astype(BF)
    up_grad = (hidden_grad * gate_pre * sigmoid_gate).astype(BF)
    gate_grad = lax.all_gather(gate_grad, "tp", axis=0, tiled=True)
    up_grad = lax.all_gather(up_grad, "tp", axis=0, tiled=True)
    hidden = lax.all_gather(hidden, "tp", axis=0, tiled=True)
    scale_high = lax.optimization_barrier(gate_scale.astype(BF))
    scale_low = (gate_scale - scale_high.astype(F32)).astype(BF)

    def weights(scale):
        per_expert = jnp.sum(jnp.where(chosen, scale.astype(F32).T[None], 0.0), axis=1)
        return jnp.where(hot, per_expert[:, None, :], 0.0).astype(BF).reshape(-1, rows)

    mix = jnp.concatenate([weights(scale_high), weights(scale_low)], axis=1)

    def combine(returned):
        both = lax.dot_general(
            mix, returned.reshape(-1, part), (((0,), (0,)), ((), ())), preferred_element_type=F32
        )
        return (both[:rows] + both[rows:]).astype(BF)

    input_grad = (dot_nt(gate_grad, gate_proj) + dot_nt(up_grad, up_proj)).astype(BF)
    returned_grad = exchange(input_grad.reshape(members, capacity, part))
    expert_out = jnp.dot(hidden, down_proj, preferred_element_type=F32).astype(BF)
    returned_out = exchange(expert_out.reshape(members, capacity, part))
    balanced_grad = combine(returned_grad)
    leaving = select_t(take, balanced_grad)
    arriving = exchange(leaving.reshape(members, per_peer, part))
    grad_rows = select_t(spread, arriving.reshape(-1, part))
    layer_out = combine(returned_out)
    return (layer_out, grad_rows)


def solution(mesh):
    placed = (
        P("dp", "tp"),
        P("dp"),
        P("dp", None),
        P("dp", None),
        P("dp", "tp", None),
        P("dp", "tp", None),
        P("dp", None, "tp"),
        P("dp", "tp"),
    )
    return jax.shard_map(
        on_device,
        mesh=mesh,
        in_specs=placed,
        out_specs=(P("dp", "tp"), P("dp", "tp")),
        check_vma=False,
    )
```

profile of v0, /device:TPU:1, one launch (start us, length us, event | category | flops | bytes accessed | tf_op | source)
XLA Modules:
  0.0 430.1 jit_solution(9517103195963572123)
XLA Ops:
  7.2 0.9 fusion.30
  8.6 1.7 convolution_convert_fusion.4
  10.3 39.3 %all_to_all.30 = bf16[32,40,896]{2,1,0:T(8,128)(2,1)S(1)} all-to-all(bf16[32,40,896]{2,1,0:T(8,128)(2,1)S(1)} %bitcast.73), channel_id=1, replica_groups=mesh['dp'=32,'tp'=8] {'dp'}, dimensions={0} | all-to-all | bytes 4587520 | tf_op jit(solution)/shard_map/all_to_all | solution.py:38
  49.6 4.3 convolution_convert_fusion
  55.2 0.8 dynamic-update-slice
  56.0 10.0 %all-reduce = s32[32]{0:T(128)S(1)} all-reduce(s32[32]{0:T(128)S(1)} %dynamic-update-slice), channel_id=1, replica_groups=mesh['dp'=32,'tp'=8] {'dp'}, use_global_device_ids=true, to_apply=%add | all-reduce | flops 32 | bytes 256
  68.8 1.6 convolution_convert_fusion.7
  70.4 8.7 %all-to-all-start = ((bf16[32,16,896]{2,1,0:T(8,128)(2,1)}), bf16[32,16,896]{2,1,0:T(8,128)(2,1)S(1)}, u32[]{:S(2)}, u32[]{:S(2)}) async-start(bf16[32,16,896]{2,1,0:T(8,128)(2,1)} %bitcast.80), calls=%async_computation | async-start | bytes 1835008 | tf_op jit(solution)/shard_map/all_to_all | solution.py:38
  79.3 15.3 %all-to-all-done = bf16[32,16,896]{2,1,0:T(8,128)(2,1)S(1)} async-done(((bf16[32,16,896]{2,1,0:T(8,128)(2,1)}), bf16[32,16,896]{2,1,0:T(8,128)(2,1)S(1)}, u32[]{:S(2)}, u32[]{:S(2)}) %all-to-all-start) | async-done | bytes 917536 | tf_op jit(solution)/shard_map/all_to_all | solution.py:38
  94.6 2.5 convolution_convert_fusion.5
  97.1 34.8 %all_to_all.31 = bf16[32,40,896]{2,1,0:T(8,128)(2,1)S(1)} all-to-all(bf16[32,40,896]{2,1,0:T(8,128)(2,1)} %bitcast.72), channel_id=1, replica_groups=mesh['dp'=32,'tp'=8] {'dp'}, dimensions={0} | all-to-all | bytes 4587520 | tf_op jit(solution)/shard_map/all_to_all | solution.py:38
  131.9 1.4 copy-done.1
  133.3 4.1 convolution_convert_fusion.2
  137.5 6.6 %convolution_convert_fusion.1 = bf16[1280,1024]{1,0:T(8,128)(2,1)} fusion(bf16[1280,896]{1,0:T(8,128)(2,1)} %bitcast.76, bf16[1,896,1024]{2,1,0:T(8,128)(2,1)} %param.13), kind=kOutput, calls=%fused_computation.2 | convolution fusion | flops 2350120960 | bytes 6750208 | tf_op jit(solution)/shard_map/dot_general | solution.py:69
  144.2 32.4 %reduce-scatter.4.cloned.1.call-done = bf16[160,1024]{1,0:T(8,128)(2,1)} async-done(((bf16[1280,1024]{1,0:T(8,128)(2,1)}), bf16[160,1024]{1,0:T(8,128)(2,1)}) %reduce-scatter.4.cloned.1.call-update) | async-done | bytes 327696 | tf_op jit(solution)/shard_map/reduce_scatter | solution.py:70
  176.5 46.1 %reduce-scatter.6.cloned.1.call-done = bf16[160,1024]{1,0:T(8,128)(2,1)} async-done(((bf16[1280,1024]{1,0:T(8,128)(2,1)}), bf16[160,1024]{1,0:T(8,128)(2,1)}) %reduce-scatter.6.cloned.1.call-update) | async-done | bytes 327696 | tf_op jit(solution)/shard_map/reduce_scatter | solution.py:71
  222.6 2.5 fusion.18
  226.4 41.7 %all-gather.6.cloned.1.call-done = bf16[1280,1024]{1,0:T(8,128)(2,1)} async-done(((bf16[160,1024]{1,0:T(8,128)(2,1)}), bf16[1280,1024]{1,0:T(8,128)(2,1)}) %all-gather.6.cloned.1.call-update) | async-done | bytes 2621456 | tf_op jit(solution)/shard_map/all_gather | solution.py:79
  268.1 6.7 %fusion.4 = f32[1280,896]{1,0:T(8,128)} fusion(bf16[1280,1024]{1,0:T(8,128)(2,1)} %all-gather.6.cloned.1.call-done, bf16[1,896,1024]{2,1,0:T(8,128)(2,1)S(1)} %copy-done), kind=kOutput, calls=%fused_computation.11 | convolution fusion | flops 2348810240 | bytes 9043968 | tf_op jit(solution)/shard_map/dot_general | solution.py:25
  274.8 36.4 %all-gather.8.cloned.1.call-done = bf16[1280,1024]{1,0:T(8,128)(2,1)} async-done(((bf16[160,1024]{1,0:T(8,128)(2,1)}), bf16[1280,1024]{1,0:T(8,128)(2,1)}) %all-gather.8.cloned.1.call-update) | async-done | bytes 2621456 | tf_op jit(solution)/shard_map/all_gather | solution.py:80
  311.3 7.9 %add_convert_fusion = bf16[1280,896]{1,0:T(8,128)(2,1)} fusion(f32[1280,896]{1,0:T(8,128)} %fusion.4, bf16[1280,1024]{1,0:T(8,128)(2,1)} %all-gather.8.cloned.1.call-done, bf16[1,896,1024]{2,1,0:T(8,128)(2,1)} %param.13), kind=kOutput, calls=%fused_computation | convolution fusion | flops 2351104000 | bytes 11337728 | tf_op jit(solution)/shard_map/dot_general | solution.py:25
  319.2 10.5 %all-to-all-start.4 = ((bf16[32,40,896]{2,1,0:T(8,128)(2,1)}), bf16[32,40,896]{2,1,0:T(8,128)(2,1)}, u32[]{:S(2)}, u32[]{:S(2)}) async-start(bf16[32,40,896]{2,1,0:T(8,128)(2,1)} %bitcast.77), calls=%async_computation.7 | async-start | bytes 4587520 | tf_op jit(solution)/shard_map/all_to_all | solution.py:38
  329.7 24.2 %all-gather.4.cloned.1.call-done = bf16[1280,1024]{1,0:T(8,128)(2,1)} async-done(((bf16[160,1024]{1,0:T(8,128)(2,1)}), bf16[1280,1024]{1,0:T(8,128)(2,1)}) %all-gather.4.cloned.1.call-update) | async-done | bytes 2621456 | tf_op jit(solution)/shard_map/all_gather | solution.py:81
  353.9 6.6 %convolution_convert_fusion.3 = bf16[1280,896]{1,0:T(8,128)(2,1)} fusion(bf16[1280,1024]{1,0:T(8,128)(2,1)} %all-gather.4.cloned.1.call-done, bf16[1,1024,896]{2,1,0:T(8,128)(2,1)} %param.14), kind=kOutput, calls=%fused_computation.4 | convolution fusion | flops 2349957120 | bytes 6750208 | tf_op jit(solution)/shard_map/dot_general | solution.py:99
  360.5 10.7 %all-to-all-start.2 = ((bf16[32,40,896]{2,1,0:T(8,128)(2,1)}), bf16[32,40,896]{2,1,0:T(8,128)(2,1)}, u32[]{:S(2)}, u32[]{:S(2)}) async-start(bf16[32,40,896]{2,1,0:T(8,128)(2,1)} %bitcast.74), calls=%async_computation.4 | async-start | bytes 4587520 | tf_op jit(solution)/shard_map/all_to_all | solution.py:38
  371.8 2.5 fusion.23
  374.3 1.4 convolution_convert_fusion.6
  375.7 26.0 %all-to-all-done.2 = bf16[32,40,896]{2,1,0:T(8,128)(2,1)} async-done(((bf16[32,40,896]{2,1,0:T(8,128)(2,1)}), bf16[32,40,896]{2,1,0:T(8,128)(2,1)}, u32[]{:S(2)}, u32[]{:S(2)}) %all-to-all-start.2) | async-done | bytes 2293792 | tf_op jit(solution)/shard_map/all_to_all | solution.py:38
  401.6 4.5 %all-to-all-start.5 = ((bf16[32,16,896]{2,1,0:T(8,128)(2,1)}), bf16[32,16,896]{2,1,0:T(8,128)(2,1)S(1)}, u32[]{:S(2)}, u32[]{:S(2)}) async-start(bf16[32,16,896]{2,1,0:T(8,128)(2,1)} %bitcast.23), calls=%async_computation.8 | async-start | bytes 1835008 | tf_op jit(solution)/shard_map/all_to_all | solution.py:38
  406.1 2.5 fusion.24
  409.4 12.3 %all-to-all-done.5 = bf16[32,16,896]{2,1,0:T(8,128)(2,1)S(1)} async-done(((bf16[32,16,896]{2,1,0:T(8,128)(2,1)}), bf16[32,16,896]{2,1,0:T(8,128)(2,1)S(1)}, u32[]{:S(2)}, u32[]{:S(2)}) %all-to-all-start.5) | async-done | bytes 917536 | tf_op jit(solution)/shard_map/all_to_all | solution.py:38
  421.7 1.5 convolution_convert_fusion.8
  (52 shorter events, 6.6 us)
Async XLA Ops:
  7.2 126.1 %copy-start = (bf16[1,896,1024]{2,1,0:T(8,128)(2,1)S(1)}, bf16[1,896,1024]{2,1,0:T(8,128)(2,1)}, u32[]{:S(2)}) copy-start(bf16[1,896,1024]{2,1,0:T(8,128)(2,1)} %param.12) | copy-start | bytes 5505028
  7.2 137.0 %reduce-scatter.8.cloned.1.call-start = ((), (), s32[]{:S(2)}) async-start(), calls=%async_computation.12 | async-start | bytes 2949120 | tf_op jit(solution)/shard_map/reduce_scatter | solution.py:66
  10.3 39.3 %copy-start.4 = (bf16[1,1024,896]{2,1,0:T(8,128)(2,1)S(1)}, bf16[1,1024,896]{2,1,0:T(8,128)(2,1)}, u32[]{:S(2)}) copy-start(bf16[1,1024,896]{2,1,0:T(8,128)(2,1)} %param.14) | copy-start | bytes 5505028
  53.9 0.7 copy-start.6
  53.9 14.9 %copy-start.5 = (bf16[384,896]{1,0:T(8,128)(2,1)S(1)}, bf16[384,896]{1,0:T(8,128)(2,1)}, u32[]{:S(2)}) copy-start(bf16[384,896]{1,0:T(8,128)(2,1)} %param.8) | copy-start | bytes 2064388
  70.4 24.2 %all-to-all-start = ((bf16[32,16,896]{2,1,0:T(8,128)(2,1)}), bf16[32,16,896]{2,1,0:T(8,128)(2,1)S(1)}, u32[]{:S(2)}, u32[]{:S(2)}) async-start(bf16[32,16,896]{2,1,0:T(8,128)(2,1)} %bitcast.80), calls=%async_computation | async-start | bytes 1835008 | tf_op jit(solution)/shard_map/all_to_all | solution.py:38
  79.1 97.4 %reduce-scatter.4.cloned.1.call-start = ((), (), s32[]{:S(2)}) async-start(), calls=%async_computation.9 | async-start | bytes 2949120 | tf_op jit(solution)/shard_map/reduce_scatter | solution.py:70
  131.9 1.4 copy-start.1
  137.5 85.2 %reduce-scatter.6.cloned.1.call-start = ((), (), s32[]{:S(2)}) async-start(), calls=%async_computation.10 | async-start | bytes 2949120 | tf_op jit(solution)/shard_map/reduce_scatter | solution.py:71
  144.1 124.0 %all-gather.6.cloned.1.call-start = ((), (), s32[]{:S(2)}) async-start(), calls=%async_computation.13 | async-start | bytes 2949120 | tf_op jit(solution)/shard_map/all_gather | solution.py:79
  225.2 86.0 %all-gather.8.cloned.1.call-start = ((), (), s32[]{:S(2)}) async-start(), calls=%async_computation.14 | async-start | bytes 2949120 | tf_op jit(solution)/shard_map/all_gather | solution.py:80
  225.8 128.1 %all-gather.4.cloned.1.call-start = ((), (), s32[]{:S(2)}) async-start(), calls=%async_computation.11 | async-start | bytes 2949120 | tf_op jit(solution)/shard_map/all_gather | solution.py:81
  319.2 41.3 %all-to-all-start.4 = ((bf16[32,40,896]{2,1,0:T(8,128)(2,1)}), bf16[32,40,896]{2,1,0:T(8,128)(2,1)}, u32[]{:S(2)}, u32[]{:S(2)}) async-start(bf16[32,40,896]{2,1,0:T(8,128)(2,1)} %bitcast.77), calls=%async_computation.7 | async-start | bytes 4587520 | tf_op jit(solution)/shard_map/all_to_all | solution.py:38
  360.5 10.7 %copy-start.3 = (f32[128,8]{0,1:T(8,128)S(1)}, f32[128,8]{0,1:T(8,128)}, u32[]{:S(2)}) copy-start(f32[128,8]{0,1:T(8,128)} %param.11) | copy-start | bytes 12292
  360.5 11.0 %copy-start.2 = (s32[128,8]{0,1:T(8,128)S(1)}, s32[128,8]{0,1:T(8,128)}, u32[]{:S(2)}) copy-start(s32[128,8]{0,1:T(8,128)} %param.10) | copy-start | bytes 12292
  360.5 41.1 %all-to-all-start.2 = ((bf16[32,40,896]{2,1,0:T(8,128)(2,1)}), bf16[32,40,896]{2,1,0:T(8,128)(2,1)}, u32[]{:S(2)}, u32[]{:S(2)}) async-start(bf16[32,40,896]{2,1,0:T(8,128)(2,1)} %bitcast.74), calls=%async_computation.4 | async-start | bytes 4587520 | tf_op jit(solution)/shard_map/all_to_all | solution.py:38
  401.6 20.1 %all-to-all-start.5 = ((bf16[32,16,896]{2,1,0:T(8,128)(2,1)}), bf16[32,16,896]{2,1,0:T(8,128)(2,1)S(1)}, u32[]{:S(2)}, u32[]{:S(2)}) async-start(bf16[32,16,896]{2,1,0:T(8,128)(2,1)} %bitcast.23), calls=%async_computation.8 | async-start | bytes 1835008 | tf_op jit(solution)/shard_map/all_to_all | solution.py:38
Sparse Core Ops, SparseCore 0:
  54.0 39.0 reduce-scatter.7
  137.6 38.9 reduce-scatter.3
  179.1 43.4 reduce-scatter.5
  225.3 42.7 all-gather.5
  270.3 40.9 all-gather.7
  312.9 40.9 all-gather.3
where the time goes:
time: 431 us; the launch traced here: 430 us
  waiting for transfers between devices  235 us (55%)
  blocking collectives  84.1 us (20%)
  matrix products  50.1 us (12%)
  starting transfers between devices  34.8 us (8%)
  between operations  15 us (3%)
  other arithmetic  6.42 us (1%)
    all_to_all x2, blocking collectives, exchange(): return lax.all_to_all(tensor, 'dp', split_axis=0, concat_axis=0, tiled=True)  74.1 us
    all_to_all x4, waiting for transfers between devices, exchange(): return lax.all_to_all(tensor, 'dp', split_axis=0, concat_axis=0, tiled=True)  53.6 us
    reduce_scatter x1, waiting for transfers between devices, on_device(): up_pre = lax.psum_scatter(up_part, 'tp', scatter_dimension=0, tiled=True)  46.1 us
    all_gather x1, waiting for transfers between devices, on_device(): gate_grad = lax.all_gather(gate_grad, 'tp', axis=0, tiled=True)  41.7 us
    all_gather x1, waiting for transfers between devices, on_device(): up_grad = lax.all_gather(up_grad, 'tp', axis=0, tiled=True)  36.4 us
    all_to_all x4, starting transfers between devices, exchange(): return lax.all_to_all(tensor, 'dp', split_axis=0, concat_axis=0, tiled=True)  34.3 us
    reduce_scatter x1, waiting for transfers between devices, on_device(): lax.psum_scatter(gate_part, 'tp', scatter_dimension=0, tiled=True)  32.4 us
    all_gather x1, waiting for transfers between devices, on_device(): hidden = lax.all_gather(hidden, 'tp', axis=0, tiled=True)  24.2 us
  transfers between devices with their start and end apart: 10, of which 8 were waited for; matrix products, arithmetic and copies ran while one was open for 11% of the time, Pallas kernels for 0%

commit v1 on v0

--- a/solution.py
+++ b/solution.py
@@ -77,8 +77,11 @@
     ).astype(BF)
     up_grad = (hidden_grad * gate_pre * sigmoid_gate).astype(BF)
     gate_grad = lax.all_gather(gate_grad, "tp", axis=0, tiled=True)
-    up_grad = lax.all_gather(up_grad, "tp", axis=0, tiled=True)
-    hidden = lax.all_gather(hidden, "tp", axis=0, tiled=True)
+    up_grad, hidden = jnp.split(
+        lax.all_gather(jnp.concatenate([up_grad, hidden], axis=1), "tp", axis=0, tiled=True),
+        [up_grad.shape[1]],
+        axis=1,
+    )
     scale_high = lax.optimization_barrier(gate_scale.astype(BF))
     scale_low = (gate_scale - scale_high.astype(F32)).astype(BF)
 

time: 431 us -> 447 us (1.037)
  waiting for transfers between devices: 235 us -> 260 us
  starting transfers between devices: 34.8 us -> 26.6 us
    all_to_all x4, waiting for transfers between devices: 53.6 us -> 77.6 us  [exchange(): return lax.all_to_all(tensor, 'dp', split_axis=0, concat_axis=0, tiled=True)]
    all_to_all x4, starting transfers between devices: 34.3 us -> 26.2 us  [exchange(): return lax.all_to_all(tensor, 'dp', split_axis=0, concat_axis=0, tiled=True)]
    all_gather x2 -> x1, waiting for transfers between devices: 60.6 us -> 61.7 us  [on_device(): lax.all_gather(jnp.concatenate([up_grad, hidden], axis=1), 'tp', axis=0,...]
  transfers between devices with their start and end apart: 10 -> 9, of which waited for: 8 -> 8; matrix products, arithmetic and copies ran while one was open for 11% -> 9% of each run, Pallas kernels for 0% -> 0%
where the time goes in v1:
time: 447 us
  waiting for transfers between devices  260 us (58%)
  blocking collectives  84.2 us (19%)
  matrix products  50.1 us (11%)
  starting transfers between devices  26.6 us (6%)
  between operations  14.7 us (3%)
  other arithmetic  7.14 us (2%)
    all_to_all x4, waiting for transfers between devices, exchange(): return lax.all_to_all(tensor, 'dp', split_axis=0, concat_axis=0, tiled=True)  77.6 us
    all_to_all x2, blocking collectives, exchange(): return lax.all_to_all(tensor, 'dp', split_axis=0, concat_axis=0, tiled=True)  74.1 us
    all_gather x1, waiting for transfers between devices, on_device(): lax.all_gather(jnp.concatenate([up_grad, hidden], axis=1), 'tp', axis=0,...  61.7 us
    reduce_scatter x1, waiting for transfers between devices, on_device(): up_pre = lax.psum_scatter(up_part, 'tp', scatter_dimension=0, tiled=True)  46 us
    all_gather x1, waiting for transfers between devices, on_device(): gate_grad = lax.all_gather(gate_grad, 'tp', axis=0, tiled=True)  41.8 us
    reduce_scatter x1, waiting for transfers between devices, on_device(): lax.psum_scatter(gate_part, 'tp', scatter_dimension=0, tiled=True)  32.4 us
    all_to_all x4, starting transfers between devices, exchange(): return lax.all_to_all(tensor, 'dp', split_axis=0, concat_axis=0, tiled=True)  26.2 us
    dot_general x3, matrix products, dot_nt(): lax.dot_general(left, right, (((1,), (1,)), ((), ())), preferred_element_...  19.1 us
  transfers between devices with their start and end apart: 9, of which 8 were waited for; matrix products, arithmetic and copies ran while one was open for 9% of the time, Pallas kernels for 0%

profile of v1, /device:TPU:1, one launch (start us, length us, event | category | flops | bytes accessed | tf_op | source)
XLA Modules:
  0.0 446.5 jit_solution(14766364241612112263)
XLA Ops:
  7.2 0.9 fusion.32
  8.6 1.7 convolution_convert_fusion.5
  10.3 39.3 %all_to_all.30 = bf16[32,40,896]{2,1,0:T(8,128)(2,1)S(1)} all-to-all(bf16[32,40,896]{2,1,0:T(8,128)(2,1)S(1)} %bitcast.71), channel_id=1, replica_groups=mesh['dp'=32,'tp'=8] {'dp'}, dimensions={0} | all-to-all | bytes 4587520 | tf_op jit(solution)/shard_map/all_to_all | solution.py:38
  49.6 4.3 convolution_convert_fusion.2
  56.0 10.0 %all-reduce = s32[32]{0:T(128)S(1)} all-reduce(s32[32]{0:T(128)S(1)} %dynamic-update-slice), channel_id=1, replica_groups=mesh['dp'=32,'tp'=8] {'dp'}, use_global_device_ids=true, to_apply=%add | all-reduce | flops 32 | bytes 256
  68.8 1.6 convolution_convert_fusion.7
  70.5 8.7 %all-to-all-start.1 = ((bf16[32,16,896]{2,1,0:T(8,128)(2,1)}), bf16[32,16,896]{2,1,0:T(8,128)(2,1)S(1)}, u32[]{:S(2)}, u32[]{:S(2)}) async-start(bf16[32,16,896]{2,1,0:T(8,128)(2,1)} %bitcast.78), calls=%async_computation.2 | async-start | bytes 1835008 | tf_op jit(solution)/shard_map/all_to_all | solution.py:38
  79.3 15.3 %all-to-all-done.1 = bf16[32,16,896]{2,1,0:T(8,128)(2,1)S(1)} async-done(((bf16[32,16,896]{2,1,0:T(8,128)(2,1)}), bf16[32,16,896]{2,1,0:T(8,128)(2,1)S(1)}, u32[]{:S(2)}, u32[]{:S(2)}) %all-to-all-start.1) | async-done | bytes 917536 | tf_op jit(solution)/shard_map/all_to_all | solution.py:38
  94.6 2.5 convolution_convert_fusion.4
  97.1 34.8 %all_to_all.31 = bf16[32,40,896]{2,1,0:T(8,128)(2,1)S(1)} all-to-all(bf16[32,40,896]{2,1,0:T(8,128)(2,1)} %bitcast.70), channel_id=1, replica_groups=mesh['dp'=32,'tp'=8] {'dp'}, dimensions={0} | all-to-all | bytes 4587520 | tf_op jit(solution)/shard_map/all_to_all | solution.py:38
  131.9 1.5 copy-done.1
  133.3 4.1 convolution_convert_fusion.1
  137.5 6.6 %convolution_convert_fusion = bf16[1280,1024]{1,0:T(8,128)(2,1)} fusion(bf16[1280,896]{1,0:T(8,128)(2,1)} %bitcast.74, bf16[1,896,1024]{2,1,0:T(8,128)(2,1)} %param.13), kind=kOutput, calls=%fused_computation.1 | convolution fusion | flops 2350120960 | bytes 6750208 | tf_op jit(solution)/shard_map/dot_general | solution.py:69
  144.2 32.4 %reduce-scatter.6.cloned.1.call-done = bf16[160,1024]{1,0:T(8,128)(2,1)} async-done(((bf16[1280,1024]{1,0:T(8,128)(2,1)}), bf16[160,1024]{1,0:T(8,128)(2,1)}) %reduce-scatter.6.cloned.1.call-update) | async-done | bytes 327696 | tf_op jit(solution)/shard_map/reduce_scatter | solution.py:70
  176.6 46.0 %reduce-scatter.8.cloned.1.call-done = bf16[160,1024]{1,0:T(8,128)(2,1)} async-done(((bf16[1280,1024]{1,0:T(8,128)(2,1)}), bf16[160,1024]{1,0:T(8,128)(2,1)}) %reduce-scatter.8.cloned.1.call-update) | async-done | bytes 327696 | tf_op jit(solution)/shard_map/reduce_scatter | solution.py:71
  222.6 2.4 fusion.14
  225.2 0.9 pad_maximum_fusion.1
  226.1 41.8 %all-gather.5.cloned.1.call-done = bf16[1280,1024]{1,0:T(8,128)(2,1)} async-done(((bf16[160,1024]{1,0:T(8,128)(2,1)}), bf16[1280,1024]{1,0:T(8,128)(2,1)}) %all-gather.5.cloned.1.call-update) | async-done | bytes 2621456 | tf_op jit(solution)/shard_map/all_gather | solution.py:79
  267.9 6.8 %fusion.4 = f32[1280,896]{1,0:T(8,128)} fusion(bf16[1280,1024]{1,0:T(8,128)(2,1)} %all-gather.5.cloned.1.call-done, bf16[1,896,1024]{2,1,0:T(8,128)(2,1)S(1)} %copy-done), kind=kOutput, calls=%fused_computation.11 | convolution fusion | flops 2348810240 | bytes 9043968 | tf_op jit(solution)/shard_map/dot_general | solution.py:25
  274.7 61.7 %all-gather.3.cloned.1.call-done = bf16[1280,2048]{1,0:T(8,128)(2,1)} async-done(((bf16[160,2048]{1,0:T(8,128)(2,1)}), bf16[1280,2048]{1,0:T(8,128)(2,1)}) %all-gather.3.cloned.1.call-update) | async-done | bytes 5242896 | tf_op jit(solution)/shard_map/all_gather | solution.py:81
  336.4 8.0 %add_convert_fusion = bf16[1280,896]{1,0:T(8,128)(2,1)} fusion(f32[1280,896]{1,0:T(8,128)} %fusion.4, bf16[1280,2048]{1,0:T(8,128)(2,1)} %all-gather.3.cloned.1.call-done, bf16[1,896,1024]{2,1,0:T(8,128)(2,1)} %param.13), kind=kOutput, calls=%fused_computation | convolution fusion | flops 2351104000 | bytes 11337728 | tf_op jit(solution)/shard_map/dot_general | solution.py:25
  344.4 7.6 %all-to-all-start.4 = ((bf16[32,40,896]{2,1,0:T(8,128)(2,1)}), bf16[32,40,896]{2,1,0:T(8,128)(2,1)}, u32[]{:S(2)}, u32[]{:S(2)}) async-start(bf16[32,40,896]{2,1,0:T(8,128)(2,1)} %bitcast.75), calls=%async_computation.7 | async-start | bytes 4587520 | tf_op jit(solution)/shard_map/all_to_all | solution.py:38
  351.9 6.6 %convolution_convert_fusion.3 = bf16[1280,896]{1,0:T(8,128)(2,1)} fusion(bf16[1280,2048]{1,0:T(8,128)(2,1)} %all-gather.3.cloned.1.call-done, bf16[1,1024,896]{2,1,0:T(8,128)(2,1)} %param.14), kind=kOutput, calls=%fused_computation.4 | convolution fusion | flops 2349957120 | bytes 6750208 | tf_op jit(solution)/shard_map/dot_general | solution.py:102
  358.5 23.9 %all-to-all-done.4 = bf16[32,40,896]{2,1,0:T(8,128)(2,1)} async-done(((bf16[32,40,896]{2,1,0:T(8,128)(2,1)}), bf16[32,40,896]{2,1,0:T(8,128)(2,1)}, u32[]{:S(2)}, u32[]{:S(2)}) %all-to-all-start.4) | async-done | bytes 2293792 | tf_op jit(solution)/shard_map/all_to_all | solution.py:38
  382.4 5.4 %all-to-all-start.3 = ((bf16[32,40,896]{2,1,0:T(8,128)(2,1)}), bf16[32,40,896]{2,1,0:T(8,128)(2,1)}, u32[]{:S(2)}, u32[]{:S(2)}) async-start(bf16[32,40,896]{2,1,0:T(8,128)(2,1)} %bitcast.72), calls=%async_computation.6 | async-start | bytes 4587520 | tf_op jit(solution)/shard_map/all_to_all | solution.py:38
  388.5 2.5 fusion.25
  391.0 1.3 convolution_convert_fusion.6
  392.3 26.1 %all-to-all-done.3 = bf16[32,40,896]{2,1,0:T(8,128)(2,1)} async-done(((bf16[32,40,896]{2,1,0:T(8,128)(2,1)}), bf16[32,40,896]{2,1,0:T(8,128)(2,1)}, u32[]{:S(2)}, u32[]{:S(2)}) %all-to-all-start.3) | async-done | bytes 2293792 | tf_op jit(solution)/shard_map/all_to_all | solution.py:38
  418.4 4.5 %all-to-all-start.5 = ((bf16[32,16,896]{2,1,0:T(8,128)(2,1)}), bf16[32,16,896]{2,1,0:T(8,128)(2,1)S(1)}, u32[]{:S(2)}, u32[]{:S(2)}) async-start(bf16[32,16,896]{2,1,0:T(8,128)(2,1)} %bitcast.23), calls=%async_computation.8 | async-start | bytes 1835008 | tf_op jit(solution)/shard_map/all_to_all | solution.py:38
  422.9 2.5 fusion.26
  426.2 12.3 %all-to-all-done.5 = bf16[32,16,896]{2,1,0:T(8,128)(2,1)S(1)} async-done(((bf16[32,16,896]{2,1,0:T(8,128)(2,1)}), bf16[32,16,896]{2,1,0:T(8,128)(2,1)S(1)}, u32[]{:S(2)}, u32[]{:S(2)}) %all-to-all-start.5) | async-done | bytes 917536 | tf_op jit(solution)/shard_map/all_to_all | solution.py:38
  438.5 1.5 convolution_convert_fusion.8
  (50 shorter events, 6.4 us)
Async XLA Ops:
  7.2 126.2 %copy-start = (bf16[1,896,1024]{2,1,0:T(8,128)(2,1)S(1)}, bf16[1,896,1024]{2,1,0:T(8,128)(2,1)}, u32[]{:S(2)}) copy-start(bf16[1,896,1024]{2,1,0:T(8,128)(2,1)} %param.12) | copy-start | bytes 5505028
  7.2 137.0 %reduce-scatter.4.cloned.1.call-start = ((), (), s32[]{:S(2)}) async-start(), calls=%async_computation.9 | async-start | bytes 2949120 | tf_op jit(solution)/shard_map/reduce_scatter | solution.py:66
  10.3 39.3 %copy-start.4 = (bf16[1,1024,896]{2,1,0:T(8,128)(2,1)S(1)}, bf16[1,1024,896]{2,1,0:T(8,128)(2,1)}, u32[]{:S(2)}) copy-start(bf16[1,1024,896]{2,1,0:T(8,128)(2,1)} %param.14) | copy-start | bytes 5505028
  53.9 0.7 copy-start.6
  53.9 14.9 %copy-start.5 = (bf16[384,896]{1,0:T(8,128)(2,1)S(1)}, bf16[384,896]{1,0:T(8,128)(2,1)}, u32[]{:S(2)}) copy-start(bf16[384,896]{1,0:T(8,128)(2,1)} %param.8) | copy-start | bytes 2064388
  70.5 24.2 %all-to-all-start.1 = ((bf16[32,16,896]{2,1,0:T(8,128)(2,1)}), bf16[32,16,896]{2,1,0:T(8,128)(2,1)S(1)}, u32[]{:S(2)}, u32[]{:S(2)}) async-start(bf16[32,16,896]{2,1,0:T(8,128)(2,1)} %bitcast.78), calls=%async_computation.2 | async-start | bytes 1835008 | tf_op jit(solution)/shard_map/all_to_all | solution.py:38
  79.1 97.5 %reduce-scatter.6.cloned.1.call-start = ((), (), s32[]{:S(2)}) async-start(), calls=%async_computation.10 | async-start | bytes 2949120 | tf_op jit(solution)/shard_map/reduce_scatter | solution.py:70
  131.9 1.5 copy-start.1
  137.5 85.1 %reduce-scatter.8.cloned.1.call-start = ((), (), s32[]{:S(2)}) async-start(), calls=%async_computation.11 | async-start | bytes 2949120 | tf_op jit(solution)/shard_map/reduce_scatter | solution.py:71
  144.1 123.8 %all-gather.5.cloned.1.call-start = ((), (), s32[]{:S(2)}) async-start(), calls=%async_computation.13 | async-start | bytes 2949120 | tf_op jit(solution)/shard_map/all_gather | solution.py:79
  225.0 111.4 %all-gather.3.cloned.1.call-start = ((), (), s32[]{:S(2)}) async-start(), calls=%async_computation.12 | async-start | bytes 5898240 | tf_op jit(solution)/shard_map/all_gather | solution.py:81
  344.4 38.1 %all-to-all-start.4 = ((bf16[32,40,896]{2,1,0:T(8,128)(2,1)}), bf16[32,40,896]{2,1,0:T(8,128)(2,1)}, u32[]{:S(2)}, u32[]{:S(2)}) async-start(bf16[32,40,896]{2,1,0:T(8,128)(2,1)} %bitcast.75), calls=%async_computation.7 | async-start | bytes 4587520 | tf_op jit(solution)/shard_map/all_to_all | solution.py:38
  382.4 5.4 %copy-start.3 = (f32[128,8]{0,1:T(8,128)S(1)}, f32[128,8]{0,1:T(8,128)}, u32[]{:S(2)}) copy-start(f32[128,8]{0,1:T(8,128)} %param.11) | copy-start | bytes 12292
  382.4 5.7 %copy-start.2 = (s32[128,8]{0,1:T(8,128)S(1)}, s32[128,8]{0,1:T(8,128)}, u32[]{:S(2)}) copy-start(s32[128,8]{0,1:T(8,128)} %param.10) | copy-start | bytes 12292
  382.4 36.0 %all-to-all-start.3 = ((bf16[32,40,896]{2,1,0:T(8,128)(2,1)}), bf16[32,40,896]{2,1,0:T(8,128)(2,1)}, u32[]{:S(2)}, u32[]{:S(2)}) async-start(bf16[32,40,896]{2,1,0:T(8,128)(2,1)} %bitcast.72), calls=%async_computation.6 | async-start | bytes 4587520 | tf_op jit(solution)/shard_map/all_to_all | solution.py:38
  418.4 20.1 %all-to-all-start.5 = ((bf16[32,16,896]{2,1,0:T(8,128)(2,1)}), bf16[32,16,896]{2,1,0:T(8,128)(2,1)S(1)}, u32[]{:S(2)}, u32[]{:S(2)}) async-start(bf16[32,16,896]{2,1,0:T(8,128)(2,1)} %bitcast.23), calls=%async_computation.8 | async-start | bytes 1835008 | tf_op jit(solution)/shard_map/all_to_all | solution.py:38
Sparse Core Ops, SparseCore 0:
  54.0 39.0 reduce-scatter.3
  137.6 38.9 reduce-scatter.5
  179.2 43.3 reduce-scatter.7
  225.1 42.8 all-gather.4
  270.1 66.2 all-gather.2
